TPU v7x, 1024 devices: a whole 4x8x16 slice. The times are simulated.
1024 devices in a mesh: section: 8 (over y_lo, x), seq: 128 (over y_hi, z, core).
Axes of the slice: x: 4, y: 8 (y_hi: 4, y_lo: 2; y = y_hi * 2 + y_lo), z: 16, core: 2. Of those that a mesh axis runs over, the one named last changes fastest.
Arguments:
- queries: bfloat16 [8, 16384, 4096], P('section', 'seq'), may hold values from -120 to 120
- grad_out: bfloat16 [8, 16384, 4096], P('section', 'seq'), may hold values from -6 to 6
- keys: bfloat16 [16384, 1024], P('seq', 'section'), may hold values from -5.5 to 5.5
- values: bfloat16 [16384, 1024], P('seq', 'section'), may hold values from -6 to 6
- key_first: int32 [128], P('seq'), may hold values from 0 to 127, as said below
Outputs:
- grad_queries: bfloat16 [8, 16384, 4096], P('section', 'seq')
- grad_keys: float32 [16384, 1024], P('seq', 'section')
- grad_values: float32 [16384, 1024], P('seq', 'section')
Inputs may be any that keep to these rules, and one draw needn't show every extreme that they name: s - 1 <= key_first[s] <= s and key_first[s] >= 0; in every draw some shard s >= 1 has key_first[s] = s - 1.
All inputs are finite; a program needn't handle non-finite values.
Results may differ from a plain program's by a relative error of at most 0.008.
Values may be sent and summed in bfloat16 or wider, within the bound.
A program may use at most 64 MiB of HBM per device.

v0:
```python
import math

import jax
import jax.numpy as jnp
from jax import lax
from jax.sharding import PartitionSpec as P

HEADS = 32
KV_HEADS = 8
HEAD_DIM = 128
SPAN = 2


masked_score = -1e30


def passed_along(x, axis, by):
    size = lax.axis_size(axis)
    pairs = [(i, i + by) for i in range(size) if 0 <= i + by < size]
    return lax.ppermute(x, axis, pairs)


def group_grads(q_group, g_group, k_group, v_group, visible):
    score_scale = 1.0 / math.sqrt(HEAD_DIM)
    tok_rows = q_group.shape[0]
    scores = (
        jnp.einsum("igd,td->git", q_group, k_group, preferred_element_type=jnp.float32)
        * score_scale
    )
    scores = jnp.where(visible[None], scores, masked_score)
    row_max = jnp.max(scores, axis=-1, keepdims=True)
    weights = jnp.exp(scores - row_max)
    weights = weights / jnp.sum(weights, axis=-1, keepdims=True)
    dprob = jnp.einsum("igd,td->git", g_group, v_group, preferred_element_type=jnp.float32)
    row_dot = jnp.sum(weights * dprob, axis=-1, keepdims=True)
    dscore = (weights * (dprob - row_dot) * score_scale).astype(jnp.bfloat16)
    wround = weights.astype(jnp.bfloat16)
    dq_group = jnp.einsum("git,td->igd", dscore, k_group, preferred_element_type=jnp.float32)
    dq_group = dq_group.reshape(tok_rows, q_group.shape[1] * HEAD_DIM).astype(jnp.bfloat16)
    dk_group = jnp.einsum("git,igd->td", dscore, q_group, preferred_element_type=jnp.float32)
    dv_group = jnp.einsum("git,igd->td", wround, g_group, preferred_element_type=jnp.float32)
    return (dq_group, dk_group, dv_group)


def layer_grads(q_mat, g_mat, window, visible):
    tok_rows = q_mat.shape[0]
    group_size = HEADS // KV_HEADS
    head_count = window.shape[2] // HEAD_DIM
    dq_parts, dk_parts, dv_parts = ([], [], [])
    for head_kv in range(head_count):
        low = head_kv * group_size * HEAD_DIM
        high = low + group_size * HEAD_DIM
        q_group = q_mat[:, low:high].reshape(tok_rows, group_size, HEAD_DIM)
        g_group = g_mat[:, low:high].reshape(tok_rows, group_size, HEAD_DIM)
        k_group = window[0][:, head_kv * HEAD_DIM : (head_kv + 1) * HEAD_DIM]
        v_group = window[1][:, head_kv * HEAD_DIM : (head_kv + 1) * HEAD_DIM]
        dq_group, dk_group, dv_group = group_grads(q_group, g_group, k_group, v_group, visible)
        dq_parts.append(dq_group)
        dk_parts.append(dk_group)
        dv_parts.append(dv_group)
    grads = jnp.stack([jnp.concatenate(dk_parts, axis=1), jnp.concatenate(dv_parts, axis=1)])
    return (jnp.concatenate(dq_parts, axis=1), grads)


def body(queries, grad_out, keys, values, key_first):
    tok_rows = keys.shape[0]
    shard_index = lax.axis_index("seq")
    key_start = key_first[0]
    cache_pair = jnp.stack([keys, values])
    key_count = SPAN * tok_rows
    q_pos = shard_index * tok_rows + jnp.arange(tok_rows, dtype=jnp.int32)
    k_pos = (shard_index - SPAN + 1) * tok_rows + jnp.arange(key_count, dtype=jnp.int32)
    visible = (k_pos[None, :] >= key_start * tok_rows) & (k_pos[None, :] <= q_pos[:, None])
    gathered = lax.all_gather(cache_pair, "section", axis=2, tiled=True)
    pieces = [gathered]
    offset = 1
    pieces.insert(0, passed_along(gathered, "seq", offset))
    window = jnp.concatenate(pieces, axis=1)
    dq_layer, grads = layer_grads(queries[0], grad_out[0], window, visible)
    grad_queries = dq_layer[None]
    grads = grads.reshape(2, SPAN, tok_rows, grads.shape[2])
    summed = grads[:, SPAN - 1]
    offset = 1
    summed = summed + passed_along(
        grads[:, SPAN - 1 - offset].astype(jnp.bfloat16), "seq", -offset
    ).astype(jnp.float32)
    owned = lax.psum_scatter(summed, "section", scatter_dimension=2, tiled=True)
    return (grad_queries, owned[0], owned[1])


def solution(mesh):
    placed = (
        P("section", "seq", None),
        P("section", "seq", None),
        P("seq", "section"),
        P("seq", "section"),
        P("seq"),
    )
    return jax.shard_map(
        body,
        mesh=mesh,
        in_specs=placed,
        out_specs=(P("section", "seq", None), P("seq", "section"), P("seq", "section")),
        check_vma=False,
    )
```

profile of v0, /device:TPU:56, one launch (start us, length us, event | category | flops | bytes accessed | tf_op | source)
XLA Modules:
  0.0 178.4 jit_solution(2400479612961738995)
XLA Ops:
  8.0 26.0 %all_gather.3 = bf16[2,128,1024]{2,1,0:T(8,128)(2,1)S(1)} all-gather(bf16[2,128,128]{2,1,0:T(8,128)(2,1)S(1)} %pad_maximum_fusion.1), channel_id=1, replica_groups=mesh['section'=8,'seq'=128] {'section'}, dimensions={2}, use_global_device_ids=true | all-gather | bytes 589824 | tf_op jit(solution)/shard_map/all_gather | solution.py:74
  34.0 1.9 %collective-permute-start = (bf16[2,128,1024]{2,1,0:T(8,128)(2,1)S(1)}, bf16[2,128,1024]{2,1,0:T(8,128)(2,1)S(1)}, u32[]{:S(2)}, u32[]{:S(2)}) collective-permute-start(bf16[2,128,1024]{2,1,0:T(8,128)(2,1)S(1)} %all_gather.3), channel_id=1, source_target_pairs={{0,1},{1,2},{2,3},{3,4},{4,5},{5,6},{6,7},{7,8},{8,9},{9,10},{10,1... | collective-permute-start | bytes 1572872 | tf_op jit(solution)/shard_map/ppermute | solution.py:20
  37.4 1.6 copy.66
  39.0 1.6 copy.68
  41.7 19.4 %collective-permute-done = bf16[2,128,1024]{2,1,0:T(8,128)(2,1)S(1)} collective-permute-done((bf16[2,128,1024]{2,1,0:T(8,128)(2,1)S(1)}, bf16[2,128,1024]{2,1,0:T(8,128)(2,1)S(1)}, u32[]{:S(2)}, u32[]{:S(2)}) %collective-permute-start) | collective-permute-done | bytes 524320 | tf_op jit(solution)/shard_map/ppermute | solution.py:20
  62.1 1.7 fusion.215
  63.8 1.7 fusion.216
  65.5 1.6 fusion.217
  67.1 1.7 fusion.218
  68.8 1.1 fusion.219
  69.9 1.1 fusion.220
  71.0 1.1 fusion.221
  72.1 1.1 fusion.222
  73.2 1.3 fusion.87
  74.5 1.0 convolution_bitcast_fusion.7
  75.6 1.1 convolution_bitcast_fusion.6
  77.6 1.0 convolution_bitcast_fusion.4
  78.7 1.0 convolution_bitcast_fusion.3
  79.7 1.0 convolution_bitcast_fusion.2
  82.0 1.7 fusion.86
  83.7 1.3 fusion.85
  85.0 1.3 fusion.84
  86.4 1.3 fusion.83
  87.7 1.3 fusion.82
  89.0 1.3 fusion.81
  90.4 1.3 fusion.80
  92.6 2.5 %fusion.95 = f32[256,1024]{0,1:T(8,128)} fusion(bf16[128,4,128]{0,2,1:T(8,128)(2,1)S(1)} %bitcast.483, f32[4,128,256]{1,2,0:T(8,128)} %convolution_bitcast_fusion.7, f32[4,128,256]{1,2,0:T(8,128)} %get-tuple-element.24, f32[4,128]{1,0:T(4,128)} %get-tuple-element.23), kind=kOutput, calls=%fused_computation.137 | convolution fusion | flops 34472704 | bytes 2363392 | tf_op jit(solution)/shard_map/git,igd->td/dot_general | solution.py:40
  95.1 2.5 %fusion.94 = f32[256,1024]{0,1:T(8,128)} fusion(f32[256,1024]{0,1:T(8,128)} %fusion.95, bf16[128,4,128]{0,2,1:T(8,128)(2,1)S(1)} %bitcast.480, f32[4,128,256]{1,2,0:T(8,128)} %convolution_bitcast_fusion.6, f32[4,128,256]{1,2,0:T(8,128)} %get-tuple-element.26, f32[4,128]{1,0:T(4,128)S(1)} %copy-done.31), kind=kOutput, calls=%fused_computation.135 | convolution fusion | flops 34472704 | bytes 2363392 | tf_op jit(solution)/shard_map/git,igd->td/dot_general | solution.py:40
  97.7 2.5 %fusion.93 = f32[256,1024]{0,1:T(8,128)} fusion(f32[256,1024]{0,1:T(8,128)} %fusion.94, bf16[128,4,128]{0,2,1:T(8,128)(2,1)S(1)} %bitcast.477, f32[4,128,256]{1,2,0:T(8,128)} %convolution_bitcast_fusion.5, f32[4,128,256]{1,2,0:T(8,128)} %get-tuple-element.28, f32[4,128]{1,0:T(4,128)S(1)} %copy-done.27), kind=kOutput, calls=%fused_computation.133 | convolution fusion | flops 34472704 | bytes 2363392 | tf_op jit(solution)/shard_map/git,igd->td/dot_general | solution.py:40
  100.1 2.6 %fusion.92 = f32[256,1024]{0,1:T(8,128)} fusion(f32[256,1024]{0,1:T(8,128)} %fusion.93, bf16[128,4,128]{0,2,1:T(8,128)(2,1)S(1)} %bitcast.474, f32[4,128,256]{1,2,0:T(8,128)} %convolution_bitcast_fusion.4, f32[4,128,256]{1,2,0:T(8,128)} %get-tuple-element.30, f32[4,128]{1,0:T(4,128)S(1)} %copy-done.24), kind=kOutput, calls=%fused_computation.131 | convolution fusion | flops 34472704 | bytes 2363392 | tf_op jit(solution)/shard_map/git,igd->td/dot_general | solution.py:40
  102.7 2.5 %fusion.91 = f32[256,1024]{0,1:T(8,128)} fusion(f32[256,1024]{0,1:T(8,128)} %fusion.92, bf16[128,4,128]{0,2,1:T(8,128)(2,1)S(1)} %bitcast.471, f32[4,128,256]{1,2,0:T(8,128)} %convolution_bitcast_fusion.3, f32[4,128,256]{1,2,0:T(8,128)} %get-tuple-element.32, f32[4,128]{1,0:T(4,128)S(1)} %get-tuple-element.31), kind=kOutput, calls=%fused_computation.129 | convolution fusion | flops 34472704 | bytes 2363392 | tf_op jit(solution)/shard_map/git,igd->td/dot_general | solution.py:40
  105.3 2.5 %fusion.90 = f32[256,1024]{0,1:T(8,128)} fusion(f32[256,1024]{0,1:T(8,128)} %fusion.91, bf16[128,4,128]{0,2,1:T(8,128)(2,1)S(1)} %bitcast.468, f32[4,128,256]{1,2,0:T(8,128)} %convolution_bitcast_fusion.2, f32[4,128,256]{1,2,0:T(8,128)} %get-tuple-element.34, f32[4,128]{1,0:T(4,128)S(1)} %get-tuple-element.33), kind=kOutput, calls=%fused_computation.127 | convolution fusion | flops 34472704 | bytes 2363392 | tf_op jit(solution)/shard_map/git,igd->td/dot_general | solution.py:40
  107.8 2.5 %fusion.89 = f32[256,1024]{0,1:T(8,128)} fusion(f32[256,1024]{0,1:T(8,128)} %fusion.90, bf16[128,4,128]{0,2,1:T(8,128)(2,1)S(1)} %bitcast.465, f32[4,128,256]{1,2,0:T(8,128)} %convolution_bitcast_fusion.1, f32[4,128,256]{1,2,0:T(8,128)} %get-tuple-element.36, f32[4,128]{1,0:T(4,128)S(1)} %get-tuple-element.35), kind=kOutput, calls=%fused_computation.125 | convolution fusion | flops 34472704 | bytes 2363392 | tf_op jit(solution)/shard_map/git,igd->td/dot_general | solution.py:40
  110.3 2.2 %fusion.88 = f32[256,1024]{0,1:T(8,128)} fusion(f32[256,1024]{0,1:T(8,128)} %fusion.89, bf16[128,4,128]{0,2,1:T(8,128)(2,1)S(1)} %bitcast.462, f32[4,128,256]{1,2,0:T(8,128)S(1)} %convolution_bitcast_fusion, f32[4,128,256]{1,2,0:T(8,128)} %get-tuple-element.38, f32[4,128]{1,0:T(4,128)S(1)} %get-tuple-element.37), kind=kOutput, calls=%fused_computation.123 | convolution fusion | flops 34472704 | bytes 2363392 | tf_op jit(solution)/shard_map/git,igd->td/dot_general | solution.py:40
  112.5 1.6 copy.182
  114.1 2.1 %collective-permute-start.1 = (bf16[2,128,1024]{2,1,0:T(8,128)(2,1)S(1)}, bf16[2,128,1024]{2,1,0:T(8,128)(2,1)S(1)}, u32[]{:S(2)}, u32[]{:S(2)}) collective-permute-start(bf16[2,128,1024]{2,1,0:T(8,128)(2,1)S(1)} %fusion.132), channel_id=1, source_target_pairs={{1,0},{2,1},{3,2},{4,3},{5,4},{6,5},{7,6},{8,7},{9,8},{10,9},{11,1... | collective-permute-start | bytes 1572872 | tf_op jit(solution)/shard_map/ppermute | solution.py:20
  116.2 1.8 %convolution_convert_fusion.6 = bf16[128,4,128]{2,0,1:T(8,128)(2,1)S(1)} fusion(f32[4,128,256]{1,2,0:T(8,128)} %convolution_bitcast_fusion.6, bf16[256,1024]{1,0:T(8,128)(2,1)} %copy-done.1, f32[4,128,256]{1,2,0:T(8,128)} %get-tuple-element.26, f32[4,128]{1,0:T(4,128)S(1)} %copy-done.32), kind=kOutput, calls=%fused_computation.104 | convolution fusion | flops 34538240 | bytes 2297856 | tf_op jit(solution)/shard_map/git,td->igd/dot_general | solution.py:38
  118.1 1.9 %convolution_convert_fusion.7 = bf16[128,4,128]{2,0,1:T(8,128)(2,1)S(1)} fusion(f32[4,128,256]{1,2,0:T(8,128)} %convolution_bitcast_fusion.7, bf16[256,1024]{1,0:T(8,128)(2,1)} %copy-done.1, f32[4,128,256]{1,2,0:T(8,128)} %get-tuple-element.24, f32[4,128]{1,0:T(4,128)S(1)} %copy-done.30), kind=kOutput, calls=%fused_computation.105 | convolution fusion | flops 34538240 | bytes 2297856 | tf_op jit(solution)/shard_map/git,td->igd/dot_general | solution.py:38
  120.0 5.4 %collective-permute-done.1 = bf16[2,128,1024]{2,1,0:T(8,128)(2,1)S(1)} collective-permute-done((bf16[2,128,1024]{2,1,0:T(8,128)(2,1)S(1)}, bf16[2,128,1024]{2,1,0:T(8,128)(2,1)S(1)}, u32[]{:S(2)}, u32[]{:S(2)}) %collective-permute-start.1) | collective-permute-done | bytes 524320 | tf_op jit(solution)/shard_map/ppermute | solution.py:20
  125.4 1.1 fusion.98
  127.6 1.8 %convolution_convert_fusion.5 = bf16[128,4,128]{2,0,1:T(8,128)(2,1)S(1)} fusion(f32[4,128,256]{1,2,0:T(8,128)} %convolution_bitcast_fusion.5, bf16[256,1024]{1,0:T(8,128)(2,1)S(1)} %copy-done.2, f32[4,128,256]{1,2,0:T(8,128)} %get-tuple-element.28, f32[4,128]{1,0:T(4,128)S(1)} %copy-done.28), kind=kOutput, calls=%fused_computation.103 | convolution fusion | flops 34538240 | bytes 2297856 | tf_op jit(solution)/shard_map/git,td->igd/dot_general | solution.py:38
  129.8 1.9 %convolution_convert_fusion.4 = bf16[128,4,128]{2,0,1:T(8,128)(2,1)S(1)} fusion(f32[4,128,256]{1,2,0:T(8,128)} %convolution_bitcast_fusion.4, bf16[256,1024]{1,0:T(8,128)(2,1)S(1)} %copy-done.2, f32[4,128,256]{1,2,0:T(8,128)} %get-tuple-element.30, f32[4,128]{1,0:T(4,128)S(1)} %copy-done.25), kind=kOutput, calls=%fused_computation.102 | convolution fusion | flops 34538240 | bytes 2297856 | tf_op jit(solution)/shard_map/git,td->igd/dot_general | solution.py:38
  131.8 1.9 %convolution_convert_fusion.3 = bf16[128,4,128]{2,0,1:T(8,128)(2,1)S(1)} fusion(f32[4,128,256]{1,2,0:T(8,128)} %convolution_bitcast_fusion.3, bf16[256,1024]{1,0:T(8,128)(2,1)S(1)} %copy-done.2, f32[4,128,256]{1,2,0:T(8,128)} %get-tuple-element.32, f32[4,128]{1,0:T(4,128)S(1)} %get-tuple-element.31), kind=kOutput, calls=%fused_computation.101 | convolution fusion | flops 34538240 | bytes 2297856 | tf_op jit(solution)/shard_map/git,td->igd/dot_general | solution.py:38
  133.8 1.8 %convolution_convert_fusion.2 = bf16[128,4,128]{2,0,1:T(8,128)(2,1)S(1)} fusion(f32[4,128,256]{1,2,0:T(8,128)} %convolution_bitcast_fusion.2, bf16[256,1024]{1,0:T(8,128)(2,1)S(1)} %copy-done.2, f32[4,128,256]{1,2,0:T(8,128)} %get-tuple-element.34, f32[4,128]{1,0:T(4,128)S(1)} %get-tuple-element.33), kind=kOutput, calls=%fused_computation.100 | convolution fusion | flops 34538240 | bytes 2297856 | tf_op jit(solution)/shard_map/git,td->igd/dot_general | solution.py:38
  135.8 1.9 %convolution_convert_fusion.1 = bf16[128,4,128]{2,0,1:T(8,128)(2,1)S(1)} fusion(f32[4,128,256]{1,2,0:T(8,128)} %convolution_bitcast_fusion.1, bf16[256,1024]{1,0:T(8,128)(2,1)S(1)} %copy-done.2, f32[4,128,256]{1,2,0:T(8,128)} %get-tuple-element.36, f32[4,128]{1,0:T(4,128)S(1)} %get-tuple-element.35), kind=kOutput, calls=%fused_computation.99 | convolution fusion | flops 34538240 | bytes 2297856 | tf_op jit(solution)/shard_map/git,td->igd/dot_general | solution.py:38
  137.8 1.8 %convolution_convert_fusion = bf16[128,4,128]{2,0,1:T(8,128)(2,1)S(1)} fusion(f32[4,128,256]{1,2,0:T(8,128)} %copy-done, bf16[256,1024]{1,0:T(8,128)(2,1)S(1)} %copy-done.2, f32[4,128,256]{1,2,0:T(8,128)} %get-tuple-element.38, f32[4,128]{1,0:T(4,128)S(1)} %get-tuple-element.37), kind=kOutput, calls=%fused_computation.98 | convolution fusion | flops 34538240 | bytes 2297856 | tf_op jit(solution)/shard_map/git,td->igd/dot_general | solution.py:38
  139.9 30.2 %reduce-scatter.2.cloned.1.call-done = f32[2,128,128]{2,1,0:T(8,128)} async-done(((f32[2,128,1024]{2,1,0:T(8,128)}), f32[2,128,128]{2,1,0:T(8,128)}) %reduce-scatter.2.cloned.1.call-update) | async-done | bytes 131088 | tf_op jit(solution)/shard_map/reduce_scatter | solution.py:87
  170.1 1.5 slice_bitcast_fusion.2
  (99 shorter events, 8.9 us)
Async XLA Ops:
  7.2 162.9 %reduce-scatter.2.cloned.1.call-start = ((), (), s32[]{:S(2)}) async-start(), calls=%async_computation.1 | async-start | bytes 1179648 | tf_op jit(solution)/shard_map/reduce_scatter | solution.py:87
  34.0 27.1 %collective-permute-start = (bf16[2,128,1024]{2,1,0:T(8,128)(2,1)S(1)}, bf16[2,128,1024]{2,1,0:T(8,128)(2,1)S(1)}, u32[]{:S(2)}, u32[]{:S(2)}) collective-permute-start(bf16[2,128,1024]{2,1,0:T(8,128)(2,1)S(1)} %all_gather.3), channel_id=1, source_target_pairs={{0,1},{1,2},{2,3},{3,4},{4,5},{5,6},{6,7},{7,8},{8,9},{9,10},{10,1... | collective-permute-start | bytes 1572872 | tf_op jit(solution)/shard_map/ppermute | solution.py:20
  61.2 0.9 copy-start.18
  61.2 0.9 copy-start.21
  61.3 29.1 %copy-start.1 = (bf16[256,1024]{1,0:T(8,128)(2,1)}, bf16[256,1024]{1,0:T(8,128)(2,1)S(1)}, u32[]{:S(2)}) copy-start(bf16[256,1024]{1,0:T(8,128)(2,1)S(1)} %get-tuple-element.19) | copy-start | bytes 1572868
  61.3 2.5 %copy-start.16 = (bf16[128,512]{0,1:T(8,128)(2,1)S(1)}, bf16[128,512]{0,1:T(8,128)(2,1)}, u32[]{:S(2)}) copy-start(bf16[128,512]{0,1:T(8,128)(2,1)} %get-tuple-element.9) | copy-start | bytes 393220
  62.1 3.4 %copy-start.13 = (bf16[128,512]{0,1:T(8,128)(2,1)S(1)}, bf16[128,512]{0,1:T(8,128)(2,1)}, u32[]{:S(2)}) copy-start(bf16[128,512]{0,1:T(8,128)(2,1)} %get-tuple-element.8) | copy-start | bytes 393220
  63.8 3.3 %copy-start.11 = (bf16[128,512]{0,1:T(8,128)(2,1)S(1)}, bf16[128,512]{0,1:T(8,128)(2,1)}, u32[]{:S(2)}) copy-start(bf16[128,512]{0,1:T(8,128)(2,1)} %get-tuple-element.7) | copy-start | bytes 393220
  65.5 3.3 %copy-start.9 = (bf16[128,512]{0,1:T(8,128)(2,1)S(1)}, bf16[128,512]{0,1:T(8,128)(2,1)}, u32[]{:S(2)}) copy-start(bf16[128,512]{0,1:T(8,128)(2,1)} %get-tuple-element.6) | copy-start | bytes 393220
  67.1 2.8 %copy-start.7 = (bf16[128,512]{0,1:T(8,128)(2,1)S(1)}, bf16[128,512]{0,1:T(8,128)(2,1)}, u32[]{:S(2)}) copy-start(bf16[128,512]{0,1:T(8,128)(2,1)} %get-tuple-element.5) | copy-start | bytes 393220
  68.8 2.2 %copy-start.5 = (bf16[128,512]{0,1:T(8,128)(2,1)S(1)}, bf16[128,512]{0,1:T(8,128)(2,1)}, u32[]{:S(2)}) copy-start(bf16[128,512]{0,1:T(8,128)(2,1)} %get-tuple-element.4) | copy-start | bytes 393220
  69.9 2.2 %copy-start.3 = (bf16[128,512]{0,1:T(8,128)(2,1)S(1)}, bf16[128,512]{0,1:T(8,128)(2,1)}, u32[]{:S(2)}) copy-start(bf16[128,512]{0,1:T(8,128)(2,1)} %get-tuple-element.3) | copy-start | bytes 393220
  71.0 2.2 %copy-start.19 = (bf16[128,512]{0,1:T(8,128)(2,1)S(1)}, bf16[128,512]{0,1:T(8,128)(2,1)}, u32[]{:S(2)}) copy-start(bf16[128,512]{0,1:T(8,128)(2,1)} %get-tuple-element.10) | copy-start | bytes 393220
  72.1 1.1 copy-start.29
  81.9 28.3 %copy-start = (f32[4,128,256]{1,2,0:T(8,128)}, f32[4,128,256]{1,2,0:T(8,128)S(1)}, u32[]{:S(2)}) copy-start(f32[4,128,256]{1,2,0:T(8,128)S(1)} %convolution_bitcast_fusion) | copy-start | bytes 1572868
  82.0 1.7 copy-start.14
  82.0 1.7 copy-start.26
  83.7 1.3 copy-start.12
  83.7 1.3 copy-start.23
  85.0 1.3 copy-start.10
  86.3 1.3 copy-start.8
  87.7 1.3 copy-start.6
  89.0 1.3 copy-start.4
  91.7 0.9 copy-start.20
  92.6 2.5 %copy-start.17 = (bf16[128,512]{0,1:T(8,128)(2,1)S(1)}, bf16[128,512]{0,1:T(8,128)(2,1)}, u32[]{:S(2)}) copy-start(bf16[128,512]{0,1:T(8,128)(2,1)} %get-tuple-element.9) | copy-start | bytes 393220
  92.6 2.5 %copy-start.31 = (f32[4,128]{1,0:T(4,128)S(1)}, f32[4,128]{1,0:T(4,128)}, u32[]{:S(2)}) copy-start(f32[4,128]{1,0:T(4,128)} %get-tuple-element.25) | copy-start | bytes 6148
  95.1 2.5 %copy-start.15 = (bf16[128,512]{0,1:T(8,128)(2,1)S(1)}, bf16[128,512]{0,1:T(8,128)(2,1)}, u32[]{:S(2)}) copy-start(bf16[128,512]{0,1:T(8,128)(2,1)} %get-tuple-element.8) | copy-start | bytes 393220
  95.1 2.5 %copy-start.27 = (f32[4,128]{1,0:T(4,128)S(1)}, f32[4,128]{1,0:T(4,128)}, u32[]{:S(2)}) copy-start(f32[4,128]{1,0:T(4,128)} %get-tuple-element.27) | copy-start | bytes 6148
  97.7 2.5 %copy-start.24 = (f32[4,128]{1,0:T(4,128)S(1)}, f32[4,128]{1,0:T(4,128)}, u32[]{:S(2)}) copy-start(f32[4,128]{1,0:T(4,128)} %get-tuple-element.29) | copy-start | bytes 6148
  114.0 2.2 %copy-start.32 = (f32[4,128]{1,0:T(4,128)S(1)}, f32[4,128]{1,0:T(4,128)}, u32[]{:S(2)}) copy-start(f32[4,128]{1,0:T(4,128)} %get-tuple-element.25) | copy-start | bytes 6148
  114.1 4.0 %copy-start.30 = (f32[4,128]{1,0:T(4,128)S(1)}, f32[4,128]{1,0:T(4,128)}, u32[]{:S(2)}) copy-start(f32[4,128]{1,0:T(4,128)} %get-tuple-element.23) | copy-start | bytes 6148
  114.1 11.3 %collective-permute-start.1 = (bf16[2,128,1024]{2,1,0:T(8,128)(2,1)S(1)}, bf16[2,128,1024]{2,1,0:T(8,128)(2,1)S(1)}, u32[]{:S(2)}, u32[]{:S(2)}) collective-permute-start(bf16[2,128,1024]{2,1,0:T(8,128)(2,1)S(1)} %fusion.132), channel_id=1, source_target_pairs={{1,0},{2,1},{3,2},{4,3},{5,4},{6,5},{7,6},{8,7},{9,8},{10,9},{11,1... | collective-permute-start | bytes 1572872 | tf_op jit(solution)/shard_map/ppermute | solution.py:20
  126.5 1.0 copy-start.2
  126.5 1.0 copy-start.28
  127.6 2.2 %copy-start.25 = (f32[4,128]{1,0:T(4,128)S(1)}, f32[4,128]{1,0:T(4,128)}, u32[]{:S(2)}) copy-start(f32[4,128]{1,0:T(4,128)} %get-tuple-element.29) | copy-start | bytes 6148
  139.9 31.7 %copy-start.22 = (bf16[128,4096]{1,0:T(8,128)(2,1)}, bf16[128,4096]{1,0:T(8,128)(2,1)S(1)}, u32[]{:S(2)}) copy-start(bf16[128,4096]{1,0:T(8,128)(2,1)S(1)} %constant_dynamic-update-slice_fusion.2) | copy-start | bytes 3145732
Sparse Core Ops, SparseCore 0:
  126.7 43.3 reduce-scatter.1
where the time goes:
time: 180 us; the launch traced here: 178 us
  matrix products  64 us (36%)
  waiting for transfers between devices  55 us (31%)
  blocking collectives  26 us (14%)
  between operations  15.3 us (8%)
  local copies, waits for them, and re-layouts  11.3 us (6%)
  starting transfers between devices  4.05 us (2%)
  other arithmetic  2.74 us (2%)
    reduce_scatter x1, waiting for transfers between devices, body(): owned = lax.psum_scatter(summed, 'section', scatter_dimension=2, tiled=True)  30.2 us
    all_gather x1, blocking collectives, body(): gathered = lax.all_gather(cache_pair, 'section', axis=2, tiled=True)  26 us
    ppermute x2, waiting for transfers between devices, passed_along(): return lax.ppermute(x, axis, pairs)  24.9 us
    dot_general x8, matrix products, group_grads(): jnp.einsum('git,igd->td', dscore, q_group, preferred_element_type=jnp.flo...  19.8 us
    dot_general x8, matrix products, group_grads(): jnp.einsum('git,td->igd', dscore, k_group, preferred_element_type=jnp.flo...  14.9 us
    sub x8, matrix products, group_grads(): weights = jnp.exp(scores - row_max)  11.1 us
    dot_general x8, matrix products, group_grads(): jnp.einsum('git,igd->td', wround, g_group, preferred_element_type=jnp.flo...  10.8 us
    dot_general x8, matrix products, group_grads(): jnp.einsum('igd,td->git', g_group, v_group, preferred_element_type=jnp.fl...  7.4 us
  transfers between devices with their start and end apart: 3, of which 3 were waited for; matrix products, arithmetic and copies ran while one was open for 12% of the time, Pallas kernels for 0%

commit v1 on v0

v1 whole, which is shorter than its diff:
```python
import math

import jax
import jax.numpy as jnp
from jax import lax
from jax.experimental import pallas as pl
from jax.experimental.pallas import tpu as pltpu
from jax.sharding import PartitionSpec as P

KV_HEADS = 8
GROUP = 4
HEAD_DIM = 128
TQ = 128
GROUP_WIDTH = GROUP * HEAD_DIM
MESH = pl.DeviceIdType.MESH

OFFSETS = ((0, 0), (1, 0), (0, 1), (0, 3), (1, 1), (1, 3), (0, 2), (1, 2))
AHEAD = 2
LAG = 2
HEADS_AT_ONCE = 2

masked_score = -1e30
never = 1e30


def dot(a, b, contract):
    return lax.dot_general(a, b, ((contract[:1], contract[1:]), ((), ())), preferred_element_type=jnp.float32)


def kernel(
    q_hbm, g_hbm, k_hbm, v_hbm, first_hbm,
    dq_ref, dk_ref, dv_ref,
    q_buf, g_buf, cur, prev, acc, back_out, back_in, part_out, part_in, first,
    q_sem, g_sem, own_sem, first_sem,
    cur_send, cur_recv, prev_send, prev_recv, back_send, back_recv, part_send, part_recv,
):
    section = lax.axis_index("section")
    shard = lax.axis_index("seq")
    shards = lax.axis_size("seq")
    y, x = section // 4, section % 4
    heads = [((y + dy) % 2) * 4 + (x + dx) % 4 for dy, dx in OFFSETS]
    askers = [((y + dy) % 2) * 4 + (x + 4 - dx) % 4 for dy, dx in OFFSETS]
    later = (shard + 1) % shards
    earlier = (shard + shards - 1) % shards
    steps = range(KV_HEADS)

    def columns(j):
        return pl.ds(pl.multiple_of(heads[j] * GROUP_WIDTH, GROUP_WIDTH), GROUP_WIDTH)

    own = [
        pltpu.make_async_copy(k_hbm, cur.at[0, 0], own_sem.at[0]),
        pltpu.make_async_copy(v_hbm, cur.at[0, 1], own_sem.at[1]),
    ]
    first_copy = pltpu.make_async_copy(first_hbm, first, first_sem)
    q_copies = [pltpu.make_async_copy(q_hbm.at[0, :, columns(j)], q_buf.at[j], q_sem.at[j]) for j in steps]
    g_copies = [pltpu.make_async_copy(g_hbm.at[0, :, columns(j)], g_buf.at[j], g_sem.at[j]) for j in steps]
    for copy in own:
        copy.start()
    first_copy.start()
    for j in steps:
        q_copies[j].start()
        g_copies[j].start()

    def remote(src, dst, send, recv, section_to, shard_to):
        return pltpu.make_async_remote_copy(
            src_ref=src, dst_ref=dst, send_sem=send, recv_sem=recv,
            device_id=(section_to, shard_to), device_id_type=MESH,
        )

    gathers = [remote(cur.at[0], cur.at[j], cur_send.at[j], cur_recv.at[j], askers[j], shard) for j in steps[1:]]
    gathers = [None] + gathers
    forwards = [remote(cur.at[j], prev.at[j], prev_send.at[j], prev_recv.at[j], section, later) for j in steps]
    backs = [remote(back_out.at[j], back_in.at[j], back_send.at[j], back_recv.at[j], section, earlier) for j in steps]
    parts = [remote(part_out.at[j], part_in.at[j], part_send.at[j], part_recv.at[j], heads[j], shard) for j in steps[1:]]
    parts = [None] + parts

    barrier = pltpu.get_barrier_semaphore()
    for j in steps[1:]:
        pl.semaphore_signal(barrier, inc=1, device_id=(heads[j], shard), device_id_type=MESH)
    for near in (earlier, later):
        pl.semaphore_signal(barrier, inc=1, device_id=(section, near), device_id_type=MESH)
    pl.semaphore_wait(barrier, KV_HEADS - 1 + 2)

    for copy in own:
        copy.wait()
    forwards[0].start()
    for j in steps[1:]:
        gathers[j].start()
    first_copy.wait()
    sees_earlier = first[0] < shard

    score_scale = 1.0 / math.sqrt(HEAD_DIM)
    base2_scale = score_scale * math.log2(math.e)
    key_pos = lax.broadcasted_iota(jnp.int32, (TQ, TQ), 0)
    query_pos = lax.broadcasted_iota(jnp.int32, (TQ, TQ), 1)
    causal = key_pos <= query_pos
    causal = jnp.concatenate([causal] * HEADS_AT_ONCE, axis=1)

    def compute(j):
        k_win = jnp.concatenate([prev[j, 0], cur[j, 0]], axis=0)
        v_win = jnp.concatenate([prev[j, 1], cur[j, 1]], axis=0)
        dk = dv = None
        for low in range(0, GROUP, HEADS_AT_ONCE):
            lanes = [slice(a * HEAD_DIM, (a + 1) * HEAD_DIM) for a in range(low, low + HEADS_AT_ONCE)]
            q = jnp.concatenate([q_buf[j, :, lane] for lane in lanes], axis=0)
            g = jnp.concatenate([g_buf[j, :, lane] for lane in lanes], axis=0)
            scores = dot(k_win, q, (1, 1))
            dprob = dot(v_win, g, (1, 1))
            old, new = scores[:TQ], jnp.where(causal, scores[TQ:], masked_score)
            old_max = jnp.where(sees_earlier, jnp.max(old, axis=0, keepdims=True), masked_score)
            row_max = jnp.maximum(old_max, jnp.max(new, axis=0, keepdims=True))
            old_shift = jnp.where(sees_earlier, row_max, never)
            powers = jnp.concatenate(
                [jnp.exp2((old - old_shift) * base2_scale), jnp.exp2((new - row_max) * base2_scale)], axis=0
            )
            inverse = 1.0 / jnp.sum(powers, axis=0, keepdims=True)
            weights = powers * inverse
            row_dot = jnp.sum(weights * dprob, axis=0, keepdims=True)
            dscore = (weights * ((dprob - row_dot) * score_scale)).astype(jnp.bfloat16)
            wround = weights.astype(jnp.bfloat16)
            dk_part, dv_part = dot(dscore, q, (1, 0)), dot(wround, g, (1, 0))
            dk = dk_part if dk is None else dk + dk_part
            dv = dv_part if dv is None else dv + dv_part
            dq = dot(dscore, k_win, (0, 0)).astype(jnp.bfloat16)
            for n in range(HEADS_AT_ONCE):
                at = pl.multiple_of(heads[j] * GROUP_WIDTH + (low + n) * HEAD_DIM, HEAD_DIM)
                dq_ref[0, :, pl.ds(at, HEAD_DIM)] = dq[n * TQ : (n + 1) * TQ]
        back_out[j, 0] = dk[:TQ].astype(jnp.bfloat16)
        back_out[j, 1] = dv[:TQ].astype(jnp.bfloat16)
        backs[j].start()
        acc[j, 0] = dk[TQ:]
        acc[j, 1] = dv[TQ:]

    def finish(j):
        backs[j].wait_recv()
        total = acc[j] + back_in[j].astype(jnp.float32)
        if j == 0:
            acc[j] = total
        else:
            part_out[j] = total.astype(jnp.bfloat16)
            parts[j].start()

    def pass_on(j):
        gathers[j].wait_recv()
        forwards[j].start()

    for j in range(1, AHEAD):
        pass_on(j)
    for j in steps:
        if j + AHEAD < KV_HEADS:
            pass_on(j + AHEAD)
        forwards[j].wait_recv()
        q_copies[j].wait()
        g_copies[j].wait()
        compute(j)
        if j >= LAG:
            finish(j - LAG)
    for j in range(KV_HEADS - LAG, KV_HEADS):
        finish(j)

    total = acc[0]
    for j in steps[1:]:
        parts[j].wait_recv()
        total = total + part_in[j].astype(jnp.float32)
    dk_ref[...] = total[0]
    dv_ref[...] = total[1]

    for j in steps:
        forwards[j].wait_send()
        backs[j].wait_send()
        if j > 0:
            gathers[j].wait_send()
            parts[j].wait_send()


def body(queries, grad_out, keys, values, key_first):
    rows, width = queries.shape[1:]
    block = (KV_HEADS, 2, TQ, HEAD_DIM)
    group = (KV_HEADS, rows, GROUP_WIDTH)
    pairs = math.prod((KV_HEADS, GROUP, TQ, 2 * TQ))
    return pl.pallas_call(
        kernel,
        out_shape=(
            jax.ShapeDtypeStruct(queries.shape, jnp.bfloat16),
            jax.ShapeDtypeStruct(keys.shape, jnp.float32),
            jax.ShapeDtypeStruct(values.shape, jnp.float32),
        ),
        in_specs=[pl.BlockSpec(memory_space=pltpu.HBM)] * 5,
        out_specs=[pl.BlockSpec(memory_space=pltpu.VMEM)] * 3,
        scratch_shapes=[
            pltpu.VMEM(group, jnp.bfloat16),
            pltpu.VMEM(group, jnp.bfloat16),
            pltpu.VMEM(block, jnp.bfloat16),
            pltpu.VMEM(block, jnp.bfloat16),
            pltpu.VMEM(block, jnp.float32),
            pltpu.VMEM(block, jnp.bfloat16),
            pltpu.VMEM(block, jnp.bfloat16),
            pltpu.VMEM(block, jnp.bfloat16),
            pltpu.VMEM(block, jnp.bfloat16),
            pltpu.SMEM((1,), jnp.int32),
            pltpu.SemaphoreType.DMA((KV_HEADS,)),
            pltpu.SemaphoreType.DMA((KV_HEADS,)),
            pltpu.SemaphoreType.DMA((2,)),
            pltpu.SemaphoreType.DMA,
        ]
        + [pltpu.SemaphoreType.DMA((KV_HEADS,))] * 8,
        compiler_params=pltpu.CompilerParams(
            collective_id=0, has_side_effects=True, vmem_limit_bytes=62 * 2**20
        ),
        cost_estimate=pl.CostEstimate(
            flops=10 * pairs * HEAD_DIM, transcendentals=pairs, bytes_accessed=3 * 2 * rows * width
        ),
    )(queries, grad_out, keys, values, key_first)


def solution(mesh):
    placed = (
        P("section", "seq", None),
        P("section", "seq", None),
        P("seq", "section"),
        P("seq", "section"),
        P("seq"),
    )
    return jax.shard_map(
        body,
        mesh=mesh,
        in_specs=placed,
        out_specs=(P("section", "seq", None), P("seq", "section"), P("seq", "section")),
        check_vma=False,
    )
```

time: 180 us -> 56.8 us (0.32)
  the two profiles are of different devices: /device:TPU:56 before, /device:TPU:2 now
where the time goes in v1:
time: 56.8 us; the launch traced here: 56.6 us
  Pallas kernels  51.4 us (90%)
  local copies, waits for them, and re-layouts  3.81 us (7%)
  between operations  1.3 us (2%)
    pallas_call x1, Pallas kernels, body(): pl.pallas_call(kernel, out_shape=(jax.ShapeDtypeStruct(queries.shape, jnp...  51.4 us
    unnamed x7, local copies, waits for them, and re-layouts  3.81 us

profile of v1, /device:TPU:2, one launch (start us, length us, event | category | flops | bytes accessed | tf_op | source)
XLA Modules:
  0.0 56.6 jit_solution(10513716050760660763)
XLA Ops:
  1.3 51.4 %shard_map.76 = (bf16[1,128,4096]{2,1,0:T(8,128)(2,1)}, f32[128,128]{1,0:T(8,128)}, f32[128,128]{1,0:T(8,128)}) custom-call(bf16[1,128,4096]{2,1,0:T(8,128)(2,1)} %q_hbm.1, bf16[1,128,4096]{2,1,0:T(8,128)(2,1)} %g_hbm.1, bf16[128,128]{1,0:T(8,128)(2,1)} %k_hbm.1, bf16[128,128]{1,0:T(8,128)(2,1)} %v_hbm.1, s32[1]{0:T(128)S(6)} %copy.11.first_hbm), custom_call_target="tpu_custom_call" | custom-call | flops 1342177280 | bytes 3145728 | tf_op jit(solution)/shard_map/pallas_call | solution.py:181
  52.7 0.0 copy-start.1
  52.7 2.3 %copy.12 = bf16[1,128,4096]{2,1,0:T(8,128)(2,1)} copy(bf16[1,128,4096]{2,1,0:T(8,128)(2,1)} %get-tuple-element.6) | data formatting | bytes 2097152
  55.1 0.0 copy-done.1
  55.1 0.0 copy-start
  55.1 0.6 %copy.13 = f32[128,128]{1,0:T(8,128)} copy(f32[128,128]{1,0:T(8,128)S(1)} %copy-done.1) | data formatting | bytes 131072
  55.7 0.2 copy-done
  55.9 0.6 %copy.14 = f32[128,128]{1,0:T(8,128)} copy(f32[128,128]{1,0:T(8,128)S(1)} %copy-done) | data formatting | bytes 131072
Async XLA Ops:
  52.7 2.3 %copy-start.1 = (f32[128,128]{1,0:T(8,128)S(1)}, f32[128,128]{1,0:T(8,128)}, u32[]{:S(2)}) copy-start(f32[128,128]{1,0:T(8,128)} %get-tuple-element.7) | copy-start | bytes 196612
  55.1 0.9 %copy-start = (f32[128,128]{1,0:T(8,128)S(1)}, f32[128,128]{1,0:T(8,128)}, u32[]{:S(2)}) copy-start(f32[128,128]{1,0:T(8,128)} %get-tuple-element.8) | copy-start | bytes 196612

commit v2 on v1

--- a/solution.py
+++ b/solution.py
@@ -1,3 +1,4 @@
+import functools
 import math
 
 import jax
@@ -17,7 +18,8 @@
 OFFSETS = ((0, 0), (1, 0), (0, 1), (0, 3), (1, 1), (1, 3), (0, 2), (1, 2))
 AHEAD = 2
 LAG = 2
-HEADS_AT_ONCE = 2
+RUN = 32
+HEADS_AT_ONCE = 4
 
 masked_score = -1e30
 never = 1e30
@@ -30,9 +32,11 @@
 def kernel(
     q_hbm, g_hbm, k_hbm, v_hbm, first_hbm,
     dq_ref, dk_ref, dv_ref,
-    q_buf, g_buf, cur, prev, acc, back_out, back_in, part_out, part_in, first,
+    q_buf, g_buf, cur, prev, acc, back_out, back_in, part_out, part_in,
+    edge_in, edge_out, edge_last, first,
     q_sem, g_sem, own_sem, first_sem,
-    cur_send, cur_recv, prev_send, prev_recv, back_send, back_recv, part_send, part_recv,
+    cur_send, cur_recv, forward_send, relay_send, prev_recv, back_send, back_recv, part_send, part_recv,
+    edge_send, edge_recv,
 ):
     section = lax.axis_index("section")
     shard = lax.axis_index("seq")
@@ -41,6 +45,13 @@
     heads = [((y + dy) % 2) * 4 + (x + dx) % 4 for dy, dx in OFFSETS]
     askers = [((y + dy) % 2) * 4 + (x + 4 - dx) % 4 for dy, dx in OFFSETS]
     later = (shard + 1) % shards
+    near_earlier = shard % RUN != 0
+    near_later = (shard + 1) % RUN != 0
+    has_earlier = shard > 0
+    has_later = shard < shards - 1
+    far_earlier = jnp.logical_and(has_earlier, jnp.logical_not(near_earlier))
+    far_later = jnp.logical_and(has_later, jnp.logical_not(near_later))
+    run_start = jnp.logical_not(near_earlier)
     earlier = (shard + shards - 1) % shards
     steps = range(KV_HEADS)
 
@@ -56,10 +67,6 @@
     g_copies = [pltpu.make_async_copy(g_hbm.at[0, :, columns(j)], g_buf.at[j], g_sem.at[j]) for j in steps]
     for copy in own:
         copy.start()
-    first_copy.start()
-    for j in steps:
-        q_copies[j].start()
-        g_copies[j].start()
 
     def remote(src, dst, send, recv, section_to, shard_to):
         return pltpu.make_async_remote_copy(
@@ -69,23 +76,35 @@
 
     gathers = [remote(cur.at[0], cur.at[j], cur_send.at[j], cur_recv.at[j], askers[j], shard) for j in steps[1:]]
     gathers = [None] + gathers
-    forwards = [remote(cur.at[j], prev.at[j], prev_send.at[j], prev_recv.at[j], section, later) for j in steps]
+    forwards = [remote(cur.at[j], prev.at[j], forward_send.at[j], prev_recv.at[j], section, later) for j in steps]
+    relays = [remote(prev.at[0], prev.at[j], relay_send.at[j], prev_recv.at[j], askers[j], shard) for j in steps[1:]]
+    relays = [None] + relays
     backs = [remote(back_out.at[j], back_in.at[j], back_send.at[j], back_recv.at[j], section, earlier) for j in steps]
     parts = [remote(part_out.at[j], part_in.at[j], part_send.at[j], part_recv.at[j], heads[j], shard) for j in steps[1:]]
     parts = [None] + parts
+    edges = [remote(back_out.at[j], edge_in.at[j], edge_send.at[j], edge_recv.at[j], heads[j], shard) for j in steps[1:]]
+    edges = [remote(edge_out, edge_last, edge_send.at[0], edge_recv.at[0], section, earlier)] + edges
 
     barrier = pltpu.get_barrier_semaphore()
     for j in steps[1:]:
         pl.semaphore_signal(barrier, inc=1, device_id=(heads[j], shard), device_id_type=MESH)
-    for near in (earlier, later):
-        pl.semaphore_signal(barrier, inc=1, device_id=(section, near), device_id_type=MESH)
-    pl.semaphore_wait(barrier, KV_HEADS - 1 + 2)
+
+    @pl.when(has_earlier)
+    def _():
+        pl.semaphore_signal(barrier, inc=1, device_id=(section, earlier), device_id_type=MESH)
+
+    pl.semaphore_wait(barrier, KV_HEADS - 1 + jnp.where(has_later, 1, 0))
 
     for copy in own:
         copy.wait()
-    forwards[0].start()
+    pl.when(has_later)(forwards[0].start)
+    pl.when(far_later)(forwards[0].wait_send)
     for j in steps[1:]:
         gathers[j].start()
+    first_copy.start()
+    for j in steps:
+        q_copies[j].start()
+        g_copies[j].start()
     first_copy.wait()
     sees_earlier = first[0] < shard
 
@@ -127,36 +146,69 @@
                 dq_ref[0, :, pl.ds(at, HEAD_DIM)] = dq[n * TQ : (n + 1) * TQ]
         back_out[j, 0] = dk[:TQ].astype(jnp.bfloat16)
         back_out[j, 1] = dv[:TQ].astype(jnp.bfloat16)
-        backs[j].start()
+        pl.when(near_earlier)(backs[j].start)
+        if j > 0:
+            pl.when(far_earlier)(edges[j].start)
         acc[j, 0] = dk[TQ:]
         acc[j, 1] = dv[TQ:]
 
     def finish(j):
-        backs[j].wait_recv()
-        total = acc[j] + back_in[j].astype(jnp.float32)
-        if j == 0:
-            acc[j] = total
-        else:
-            part_out[j] = total.astype(jnp.bfloat16)
+        @pl.when(near_later)
+        def _():
+            backs[j].wait_recv()
+            acc[j] += back_in[j].astype(jnp.float32)
+
+        if j > 0:
+            part_out[j] = acc[j].astype(jnp.bfloat16)
             parts[j].start()
 
     def pass_on(j):
         gathers[j].wait_recv()
-        forwards[j].start()
-
-    for j in range(1, AHEAD):
-        pass_on(j)
+        pl.when(near_later)(forwards[j].start)
+
+    @pl.when(run_start)
+    def _():
+        for j in steps[1:]:
+            pass_on(j)
+
+    @pl.when(jnp.logical_not(has_earlier))
+    def _():
+        prev[...] = jnp.zeros_like(prev)
+
+    @pl.when(far_earlier)
+    def _():
+        forwards[0].wait_recv()
+        for j in steps[1:]:
+            relays[j].start()
+
+    @pl.when(near_earlier)
+    def _():
+        for j in range(1, AHEAD):
+            pass_on(j)
+        forwards[0].wait_recv()
+
     for j in steps:
-        if j + AHEAD < KV_HEADS:
-            pass_on(j + AHEAD)
-        forwards[j].wait_recv()
+        if AHEAD <= j + AHEAD < KV_HEADS:
+            pl.when(near_earlier)(functools.partial(pass_on, j + AHEAD))
+        if j > 0:
+            pl.when(has_earlier)(forwards[j].wait_recv)
         q_copies[j].wait()
         g_copies[j].wait()
         compute(j)
+        pl.when(run_start)(functools.partial(finish, j))
         if j >= LAG:
-            finish(j - LAG)
+            pl.when(near_earlier)(functools.partial(finish, j - LAG))
     for j in range(KV_HEADS - LAG, KV_HEADS):
-        finish(j)
+        pl.when(near_earlier)(functools.partial(finish, j))
+
+    @pl.when(far_earlier)
+    def _():
+        total = back_out[0].astype(jnp.float32)
+        for j in steps[1:]:
+            edges[j].wait_recv()
+            total = total + edge_in[j].astype(jnp.float32)
+        edge_out[...] = total.astype(jnp.bfloat16)
+        edges[0].start()
 
     total = acc[0]
     for j in steps[1:]:
@@ -165,12 +217,21 @@
     dk_ref[...] = total[0]
     dv_ref[...] = total[1]
 
+    @pl.when(far_later)
+    def _():
+        edges[0].wait_recv()
+        dk_ref[...] += edge_last[0].astype(jnp.float32)
+        dv_ref[...] += edge_last[1].astype(jnp.float32)
+
+    pl.when(near_later)(forwards[0].wait_send)
     for j in steps:
-        forwards[j].wait_send()
-        backs[j].wait_send()
+        pl.when(near_earlier)(backs[j].wait_send)
+        pl.when(far_earlier)(edges[j].wait_send)
         if j > 0:
             gathers[j].wait_send()
             parts[j].wait_send()
+            pl.when(near_later)(forwards[j].wait_send)
+            pl.when(far_earlier)(relays[j].wait_send)
 
 
 def body(queries, grad_out, keys, values, key_first):
@@ -197,15 +258,18 @@
             pltpu.VMEM(block, jnp.bfloat16),
             pltpu.VMEM(block, jnp.bfloat16),
             pltpu.VMEM(block, jnp.bfloat16),
+            pltpu.VMEM(block, jnp.bfloat16),
+            pltpu.VMEM(block[1:], jnp.bfloat16),
+            pltpu.VMEM(block[1:], jnp.bfloat16),
             pltpu.SMEM((1,), jnp.int32),
             pltpu.SemaphoreType.DMA((KV_HEADS,)),
             pltpu.SemaphoreType.DMA((KV_HEADS,)),
             pltpu.SemaphoreType.DMA((2,)),
             pltpu.SemaphoreType.DMA,
         ]
-        + [pltpu.SemaphoreType.DMA((KV_HEADS,))] * 8,
+        + [pltpu.SemaphoreType.DMA((KV_HEADS,))] * 11,
         compiler_params=pltpu.CompilerParams(
-            collective_id=0, has_side_effects=True, vmem_limit_bytes=62 * 2**20
+            collective_id=0, has_side_effects=True, vmem_limit_bytes=52 * 2**20
         ),
         cost_estimate=pl.CostEstimate(
             flops=10 * pairs * HEAD_DIM, transcendentals=pairs, bytes_accessed=3 * 2 * rows * width

time: 56.8 us -> 46.3 us (0.82)
  the two profiles are of different devices: /device:TPU:2 before, /device:TPU:58 now
where the time goes in v2:
time: 46.3 us; the launch traced here: 46 us
  Pallas kernels  41 us (89%)
  local copies, waits for them, and re-layouts  3.74 us (8%)
  between operations  1.3 us (3%)
    pallas_call x1, Pallas kernels, body(): pl.pallas_call(kernel, out_shape=(jax.ShapeDtypeStruct(queries.shape, jnp...  41 us
    unnamed x7, local copies, waits for them, and re-layouts  3.74 us

profile of v2, /device:TPU:58, one launch (start us, length us, event | category | flops | bytes accessed | tf_op | source)
XLA Modules:
  0.0 46.0 jit_solution(12208038737262686203)
XLA Ops:
  1.3 0.0 copy-start
  1.3 0.7 %copy-done = bf16[128,128]{1,0:T(8,128)(2,1)S(1)} copy-done((bf16[128,128]{1,0:T(8,128)(2,1)S(1)}, bf16[128,128]{1,0:T(8,128)(2,1)}, u32[]{:S(2)}) %copy-start) | copy-done | bytes 32792
  2.0 0.0 copy-start.1
  2.0 0.8 %copy-done.1 = bf16[128,128]{1,0:T(8,128)(2,1)S(1)} copy-done((bf16[128,128]{1,0:T(8,128)(2,1)S(1)}, bf16[128,128]{1,0:T(8,128)(2,1)}, u32[]{:S(2)}) %copy-start.1) | copy-done | bytes 32792
  2.8 41.0 %shard_map.76 = (bf16[1,128,4096]{2,1,0:T(8,128)(2,1)S(1)}, f32[128,128]{1,0:T(8,128)S(1)}, f32[128,128]{1,0:T(8,128)S(1)}) custom-call(bf16[1,128,4096]{2,1,0:T(8,128)(2,1)} %q_hbm.1, bf16[1,128,4096]{2,1,0:T(8,128)(2,1)} %g_hbm.1, bf16[128,128]{1,0:T(8,128)(2,1)S(1)} %copy-done, bf16[128,128]{1,0:T(8,128)(2,1)S(1)} %copy-done.1, s32[1]{0:T(128)S(6)} %copy.11.first_hbm), custom_call_target="tpu_custom_call" | custom-call | flops 1342177280 | bytes 3145728 | tf_op jit(solution)/shard_map/pallas_call | solution.py:242
  43.8 1.0 %copy.12 = bf16[1,128,4096]{2,1,0:T(8,128)(2,1)} copy(bf16[1,128,4096]{2,1,0:T(8,128)(2,1)S(1)} %get-tuple-element.6) | data formatting | bytes 2097152
  44.8 0.6 %copy.13 = f32[128,128]{1,0:T(8,128)} copy(f32[128,128]{1,0:T(8,128)S(1)} %get-tuple-element.7) | data formatting | bytes 131072
  45.4 0.6 %copy.14 = f32[128,128]{1,0:T(8,128)} copy(f32[128,128]{1,0:T(8,128)S(1)} %get-tuple-element.8) | data formatting | bytes 131072
Async XLA Ops:
  1.3 0.8 %copy-start = (bf16[128,128]{1,0:T(8,128)(2,1)S(1)}, bf16[128,128]{1,0:T(8,128)(2,1)}, u32[]{:S(2)}) copy-start(bf16[128,128]{1,0:T(8,128)(2,1)} %k_hbm.1) | copy-start | bytes 98308
  2.0 0.8 %copy-start.1 = (bf16[128,128]{1,0:T(8,128)(2,1)S(1)}, bf16[128,128]{1,0:T(8,128)(2,1)}, u32[]{:S(2)}) copy-start(bf16[128,128]{1,0:T(8,128)(2,1)} %v_hbm.1) | copy-start | bytes 98308

commit v3 on v2

--- a/solution.py
+++ b/solution.py
@@ -19,6 +19,7 @@
 AHEAD = 2
 LAG = 2
 RUN = 32
+DIRECT_FROM = 4
 HEADS_AT_ONCE = 4
 
 masked_score = -1e30
@@ -31,7 +32,7 @@
 
 def kernel(
     q_hbm, g_hbm, k_hbm, v_hbm, first_hbm,
-    dq_ref, dk_ref, dv_ref,
+    dq_ref, dkv_ref,
     q_buf, g_buf, cur, prev, acc, back_out, back_in, part_out, part_in,
     edge_in, edge_out, edge_last, first,
     q_sem, g_sem, own_sem, first_sem,
@@ -51,7 +52,8 @@
     has_later = shard < shards - 1
     far_earlier = jnp.logical_and(has_earlier, jnp.logical_not(near_earlier))
     far_later = jnp.logical_and(has_later, jnp.logical_not(near_later))
-    run_start = jnp.logical_not(near_earlier)
+    eager = shard % RUN < 2
+    steady = jnp.logical_not(eager)
     earlier = (shard + shards - 1) % shards
     steps = range(KV_HEADS)
 
@@ -146,14 +148,14 @@
                 dq_ref[0, :, pl.ds(at, HEAD_DIM)] = dq[n * TQ : (n + 1) * TQ]
         back_out[j, 0] = dk[:TQ].astype(jnp.bfloat16)
         back_out[j, 1] = dv[:TQ].astype(jnp.bfloat16)
-        pl.when(near_earlier)(backs[j].start)
-        if j > 0:
+        pl.when(near_earlier if j < DIRECT_FROM else has_earlier)(backs[j].start)
+        if 0 < j < DIRECT_FROM:
             pl.when(far_earlier)(edges[j].start)
         acc[j, 0] = dk[TQ:]
         acc[j, 1] = dv[TQ:]
 
     def finish(j):
-        @pl.when(near_later)
+        @pl.when(near_later if j < DIRECT_FROM else has_later)
         def _():
             backs[j].wait_recv()
             acc[j] += back_in[j].astype(jnp.float32)
@@ -166,7 +168,7 @@
         gathers[j].wait_recv()
         pl.when(near_later)(forwards[j].start)
 
-    @pl.when(run_start)
+    @pl.when(eager)
     def _():
         for j in steps[1:]:
             pass_on(j)
@@ -181,30 +183,31 @@
         for j in steps[1:]:
             relays[j].start()
 
-    @pl.when(near_earlier)
+    @pl.when(steady)
     def _():
         for j in range(1, AHEAD):
             pass_on(j)
-        forwards[0].wait_recv()
+
+    pl.when(near_earlier)(forwards[0].wait_recv)
 
     for j in steps:
         if AHEAD <= j + AHEAD < KV_HEADS:
-            pl.when(near_earlier)(functools.partial(pass_on, j + AHEAD))
+            pl.when(steady)(functools.partial(pass_on, j + AHEAD))
         if j > 0:
             pl.when(has_earlier)(forwards[j].wait_recv)
         q_copies[j].wait()
         g_copies[j].wait()
         compute(j)
-        pl.when(run_start)(functools.partial(finish, j))
+        pl.when(eager)(functools.partial(finish, j))
         if j >= LAG:
-            pl.when(near_earlier)(functools.partial(finish, j - LAG))
+            pl.when(steady)(functools.partial(finish, j - LAG))
     for j in range(KV_HEADS - LAG, KV_HEADS):
-        pl.when(near_earlier)(functools.partial(finish, j))
+        pl.when(steady)(functools.partial(finish, j))
 
     @pl.when(far_earlier)
     def _():
         total = back_out[0].astype(jnp.float32)
-        for j in steps[1:]:
+        for j in range(1, DIRECT_FROM):
             edges[j].wait_recv()
             total = total + edge_in[j].astype(jnp.float32)
         edge_out[...] = total.astype(jnp.bfloat16)
@@ -214,19 +217,18 @@
     for j in steps[1:]:
         parts[j].wait_recv()
         total = total + part_in[j].astype(jnp.float32)
-    dk_ref[...] = total[0]
-    dv_ref[...] = total[1]
+    dkv_ref[...] = total
 
     @pl.when(far_later)
     def _():
         edges[0].wait_recv()
-        dk_ref[...] += edge_last[0].astype(jnp.float32)
-        dv_ref[...] += edge_last[1].astype(jnp.float32)
+        dkv_ref[...] += edge_last[...].astype(jnp.float32)
 
     pl.when(near_later)(forwards[0].wait_send)
     for j in steps:
-        pl.when(near_earlier)(backs[j].wait_send)
-        pl.when(far_earlier)(edges[j].wait_send)
+        pl.when(near_earlier if j < DIRECT_FROM else has_earlier)(backs[j].wait_send)
+        if j < DIRECT_FROM:
+            pl.when(far_earlier)(edges[j].wait_send)
         if j > 0:
             gathers[j].wait_send()
             parts[j].wait_send()
@@ -239,15 +241,14 @@
     block = (KV_HEADS, 2, TQ, HEAD_DIM)
     group = (KV_HEADS, rows, GROUP_WIDTH)
     pairs = math.prod((KV_HEADS, GROUP, TQ, 2 * TQ))
-    return pl.pallas_call(
+    grad_queries, cache_grads = pl.pallas_call(
         kernel,
         out_shape=(
-            jax.ShapeDtypeStruct(queries.shape, jnp.bfloat16),
-            jax.ShapeDtypeStruct(keys.shape, jnp.float32),
-            jax.ShapeDtypeStruct(values.shape, jnp.float32),
+            pltpu.VMEM(queries.shape, jnp.bfloat16),
+            pltpu.VMEM((2,) + keys.shape, jnp.float32),
         ),
         in_specs=[pl.BlockSpec(memory_space=pltpu.HBM)] * 5,
-        out_specs=[pl.BlockSpec(memory_space=pltpu.VMEM)] * 3,
+        out_specs=[pl.BlockSpec(memory_space=pltpu.VMEM)] * 2,
         scratch_shapes=[
             pltpu.VMEM(group, jnp.bfloat16),
             pltpu.VMEM(group, jnp.bfloat16),
@@ -269,12 +270,13 @@
         ]
         + [pltpu.SemaphoreType.DMA((KV_HEADS,))] * 11,
         compiler_params=pltpu.CompilerParams(
-            collective_id=0, has_side_effects=True, vmem_limit_bytes=52 * 2**20
+            collective_id=0, has_side_effects=True, vmem_limit_bytes=56 * 2**20
         ),
         cost_estimate=pl.CostEstimate(
             flops=10 * pairs * HEAD_DIM, transcendentals=pairs, bytes_accessed=3 * 2 * rows * width
         ),
     )(queries, grad_out, keys, values, key_first)
+    return grad_queries, cache_grads[0], cache_grads[1]
 
 
 def solution(mesh):

time: 46.3 us -> 41.1 us (0.89)
  the two profiles are of different devices: /device:TPU:58 before, /device:TPU:56 now
where the time goes in v3:
time: 41.1 us; the launch traced here: 40.9 us
  Pallas kernels  37.9 us (92%)
  local copies, waits for them, and re-layouts  1.63 us (4%)
  between operations  1.29 us (3%)
    pallas_call x1, Pallas kernels, body(): pl.pallas_call(kernel, out_shape=(pltpu.VMEM(queries.shape, jnp.bfloat16)...  37.9 us
    unnamed x1, local copies, waits for them, and re-layouts  0.97 us

profile of v3, /device:TPU:56, one launch (start us, length us, event | category | flops | bytes accessed | tf_op | source)
XLA Modules:
  0.0 40.9 jit_solution(14810915981487856740)
XLA Ops:
  1.3 37.9 %shard_map.76 = (bf16[1,128,4096]{2,1,0:T(8,128)(2,1)S(1)}, f32[2,128,128]{2,1,0:T(8,128)S(1)}) custom-call(bf16[1,128,4096]{2,1,0:T(8,128)(2,1)} %q_hbm.1, bf16[1,128,4096]{2,1,0:T(8,128)(2,1)} %g_hbm.1, bf16[128,128]{1,0:T(8,128)(2,1)} %k_hbm.1, bf16[128,128]{1,0:T(8,128)(2,1)} %v_hbm.1, s32[1]{0:T(128)S(6)} %copy.10.first_hbm), custom_call_target="tpu_custom_call" | custom-call | flops 1342177280 | bytes 3145728 | tf_op jit(solution)/shard_map/pallas_call | solution.py:244
  39.2 1.0 %copy.9 = bf16[1,128,4096]{2,1,0:T(8,128)(2,1)} copy(bf16[1,128,4096]{2,1,0:T(8,128)(2,1)S(1)} %get-tuple-element.9) | data formatting | bytes 2097152
  40.2 0.7 %slice_bitcast_fusion = (f32[128,128]{1,0:T(8,128)}, f32[128,128]{1,0:T(8,128)}) fusion(f32[2,128,128]{2,1,0:T(8,128)S(1)} %get-tuple-element.6), kind=kLoop, calls=%fused_computation | loop fusion | bytes 262144 | tf_op jit(solution)/shard_map/squeeze | solution.py:279

commit v4 on v3

--- a/solution.py
+++ b/solution.py
@@ -20,7 +20,6 @@
 LAG = 2
 RUN = 32
 DIRECT_FROM = 4
-HEADS_AT_ONCE = 4
 
 masked_score = -1e30
 never = 1e30
@@ -34,7 +33,7 @@
     q_hbm, g_hbm, k_hbm, v_hbm, first_hbm,
     dq_ref, dkv_ref,
     q_buf, g_buf, cur, prev, acc, back_out, back_in, part_out, part_in,
-    edge_in, edge_out, edge_last, first,
+    edge_in, edge_out, edge_last, own_powers, own_dprob, own_rows, first,
     q_sem, g_sem, own_sem, first_sem,
     cur_send, cur_recv, forward_send, relay_send, prev_recv, back_send, back_recv, part_send, part_recv,
     edge_send, edge_recv,
@@ -115,37 +114,51 @@
     key_pos = lax.broadcasted_iota(jnp.int32, (TQ, TQ), 0)
     query_pos = lax.broadcasted_iota(jnp.int32, (TQ, TQ), 1)
     causal = key_pos <= query_pos
-    causal = jnp.concatenate([causal] * HEADS_AT_ONCE, axis=1)
+    causal = jnp.concatenate([causal] * GROUP, axis=1)
+
+    def stacked(ref):
+        return jnp.concatenate([ref[:, a * HEAD_DIM : (a + 1) * HEAD_DIM] for a in range(GROUP)], axis=0)
+
+    def powers_of(scores, shift):
+        return jnp.exp2((scores - shift) * base2_scale)
+
+    def column_sum(x):
+        return jnp.sum(x, axis=0, keepdims=True)
+
+    def own_block(j):
+        q_copies[j].wait()
+        g_copies[j].wait()
+        scores = jnp.where(causal, dot(cur[j, 0], stacked(q_buf.at[j]), (1, 1)), masked_score)
+        dprob = dot(cur[j, 1], stacked(g_buf.at[j]), (1, 1))
+        row_max = jnp.max(scores, axis=0, keepdims=True)
+        powers = powers_of(scores, row_max)
+        own_powers[j] = powers
+        own_dprob[j] = dprob
+        own_rows[j, 0:1] = row_max
+        own_rows[j, 1:2] = column_sum(powers)
+        own_rows[j, 2:3] = column_sum(powers * dprob)
 
     def compute(j):
         k_win = jnp.concatenate([prev[j, 0], cur[j, 0]], axis=0)
-        v_win = jnp.concatenate([prev[j, 1], cur[j, 1]], axis=0)
-        dk = dv = None
-        for low in range(0, GROUP, HEADS_AT_ONCE):
-            lanes = [slice(a * HEAD_DIM, (a + 1) * HEAD_DIM) for a in range(low, low + HEADS_AT_ONCE)]
-            q = jnp.concatenate([q_buf[j, :, lane] for lane in lanes], axis=0)
-            g = jnp.concatenate([g_buf[j, :, lane] for lane in lanes], axis=0)
-            scores = dot(k_win, q, (1, 1))
-            dprob = dot(v_win, g, (1, 1))
-            old, new = scores[:TQ], jnp.where(causal, scores[TQ:], masked_score)
-            old_max = jnp.where(sees_earlier, jnp.max(old, axis=0, keepdims=True), masked_score)
-            row_max = jnp.maximum(old_max, jnp.max(new, axis=0, keepdims=True))
-            old_shift = jnp.where(sees_earlier, row_max, never)
-            powers = jnp.concatenate(
-                [jnp.exp2((old - old_shift) * base2_scale), jnp.exp2((new - row_max) * base2_scale)], axis=0
-            )
-            inverse = 1.0 / jnp.sum(powers, axis=0, keepdims=True)
-            weights = powers * inverse
-            row_dot = jnp.sum(weights * dprob, axis=0, keepdims=True)
-            dscore = (weights * ((dprob - row_dot) * score_scale)).astype(jnp.bfloat16)
-            wround = weights.astype(jnp.bfloat16)
-            dk_part, dv_part = dot(dscore, q, (1, 0)), dot(wround, g, (1, 0))
-            dk = dk_part if dk is None else dk + dk_part
-            dv = dv_part if dv is None else dv + dv_part
-            dq = dot(dscore, k_win, (0, 0)).astype(jnp.bfloat16)
-            for n in range(HEADS_AT_ONCE):
-                at = pl.multiple_of(heads[j] * GROUP_WIDTH + (low + n) * HEAD_DIM, HEAD_DIM)
-                dq_ref[0, :, pl.ds(at, HEAD_DIM)] = dq[n * TQ : (n + 1) * TQ]
+        q, g = stacked(q_buf.at[j]), stacked(g_buf.at[j])
+        old = dot(prev[j, 0], q, (1, 1))
+        old_dprob = dot(prev[j, 1], g, (1, 1))
+        own_max = own_rows[j, 0:1]
+        old_max = jnp.where(sees_earlier, jnp.max(old, axis=0, keepdims=True), masked_score)
+        row_max = jnp.maximum(old_max, own_max)
+        old_powers = powers_of(old, jnp.where(sees_earlier, row_max, never))
+        rescale = powers_of(own_max, row_max)
+        inverse = 1.0 / (rescale * own_rows[j, 1:2] + column_sum(old_powers))
+        row_dot = (rescale * own_rows[j, 2:3] + column_sum(old_powers * old_dprob)) * inverse
+        weights = jnp.concatenate([old_powers * inverse, own_powers[j] * (rescale * inverse)], axis=0)
+        dprob = jnp.concatenate([old_dprob, own_dprob[j]], axis=0)
+        dscore = (weights * ((dprob - row_dot) * score_scale)).astype(jnp.bfloat16)
+        wround = weights.astype(jnp.bfloat16)
+        dk, dv = dot(dscore, q, (1, 0)), dot(wround, g, (1, 0))
+        dq = dot(dscore, k_win, (0, 0)).astype(jnp.bfloat16)
+        for n in range(GROUP):
+            at = pl.multiple_of(heads[j] * GROUP_WIDTH + n * HEAD_DIM, HEAD_DIM)
+            dq_ref[0, :, pl.ds(at, HEAD_DIM)] = dq[n * TQ : (n + 1) * TQ]
         back_out[j, 0] = dk[:TQ].astype(jnp.bfloat16)
         back_out[j, 1] = dv[:TQ].astype(jnp.bfloat16)
         pl.when(near_earlier if j < DIRECT_FROM else has_earlier)(backs[j].start)
@@ -172,6 +185,8 @@
     def _():
         for j in steps[1:]:
             pass_on(j)
+        for j in steps:
+            own_block(j)
 
     @pl.when(jnp.logical_not(has_earlier))
     def _():
@@ -193,10 +208,9 @@
     for j in steps:
         if AHEAD <= j + AHEAD < KV_HEADS:
             pl.when(steady)(functools.partial(pass_on, j + AHEAD))
+        pl.when(steady)(functools.partial(own_block, j))
         if j > 0:
             pl.when(has_earlier)(forwards[j].wait_recv)
-        q_copies[j].wait()
-        g_copies[j].wait()
         compute(j)
         pl.when(eager)(functools.partial(finish, j))
         if j >= LAG:
@@ -262,6 +276,9 @@
             pltpu.VMEM(block, jnp.bfloat16),
             pltpu.VMEM(block[1:], jnp.bfloat16),
             pltpu.VMEM(block[1:], jnp.bfloat16),
+            pltpu.VMEM((KV_HEADS, TQ, GROUP * rows), jnp.float32),
+            pltpu.VMEM((KV_HEADS, TQ, GROUP * rows), jnp.float32),
+            pltpu.VMEM((KV_HEADS, 8, GROUP * rows), jnp.float32),
             pltpu.SMEM((1,), jnp.int32),
             pltpu.SemaphoreType.DMA((KV_HEADS,)),
             pltpu.SemaphoreType.DMA((KV_HEADS,)),

time: 41.1 us -> 40.5 us (0.985)
  Pallas kernels: 37.9 us -> 37.3 us
    pallas_call x1, Pallas kernels: 37.9 us -> 37.3 us  [body(): pl.pallas_call(kernel, out_shape=(pltpu.VMEM(queries.shape, jnp.bfloat16)...]
where the time goes in v4:
time: 40.5 us; the launch traced here: 40.3 us
  Pallas kernels  37.3 us (92%)
  local copies, waits for them, and re-layouts  1.63 us (4%)
  between operations  1.29 us (3%)
    pallas_call x1, Pallas kernels, body(): pl.pallas_call(kernel, out_shape=(pltpu.VMEM(queries.shape, jnp.bfloat16)...  37.3 us
    unnamed x1, local copies, waits for them, and re-layouts  0.97 us

profile of v4, /device:TPU:56, one launch (start us, length us, event | category | flops | bytes accessed | tf_op | source)
XLA Modules:
  0.0 40.3 jit_solution(11853102947680850834)
XLA Ops:
  1.3 37.3 %shard_map.76 = (bf16[1,128,4096]{2,1,0:T(8,128)(2,1)S(1)}, f32[2,128,128]{2,1,0:T(8,128)S(1)}) custom-call(bf16[1,128,4096]{2,1,0:T(8,128)(2,1)} %q_hbm.1, bf16[1,128,4096]{2,1,0:T(8,128)(2,1)} %g_hbm.1, bf16[128,128]{1,0:T(8,128)(2,1)} %k_hbm.1, bf16[128,128]{1,0:T(8,128)(2,1)} %v_hbm.1, s32[1]{0:T(128)S(6)} %copy.10.first_hbm), custom_call_target="tpu_custom_call" | custom-call | flops 1342177280 | bytes 3145728 | tf_op jit(solution)/shard_map/pallas_call | solution.py:258
  38.6 1.0 %copy.9 = bf16[1,128,4096]{2,1,0:T(8,128)(2,1)} copy(bf16[1,128,4096]{2,1,0:T(8,128)(2,1)S(1)} %get-tuple-element.9) | data formatting | bytes 2097152
  39.6 0.7 %slice_bitcast_fusion = (f32[128,128]{1,0:T(8,128)}, f32[128,128]{1,0:T(8,128)}) fusion(f32[2,128,128]{2,1,0:T(8,128)S(1)} %get-tuple-element.6), kind=kLoop, calls=%fused_computation | loop fusion | bytes 262144 | tf_op jit(solution)/shard_map/squeeze | solution.py:296
